TPU v7x, 32 devices: a whole 2x2x4 slice. The times are simulated.
32 devices in a mesh: row: 8 (over y, x, core), col: 4 (over z).
Axes of the slice: x: 2, y: 2, z: 4, core: 2. Of those that a mesh axis runs over, the one named last changes fastest.
Arguments:
- diag_blocks: float32 [16, 512, 512], P('row', None, 'col'), as said below
- near_blocks: float32 [16, 4, 512, 512], P('row', None, None, 'col'), may hold values from -0.1 to 0.1, as said below
- cluster_bases: float32 [16, 512, 512], P('row', 'col'), as said below
- near_ids: int32 [16, 4], P('row'), may hold values from 0 to 15, as said below
- near_count: int32 [16], P('row'), may hold values from 1 to 4
- parent_bases: float32 [8, 512, 512], P('row'), as said below
Outputs:
- leaf_diag: float32 [16, 256, 256], P('row', None, 'col')
- leaf_near: float32 [16, 4, 256, 256], P('row', None, None, 'col')
- parent_diag: float32 [8, 256, 256], P('row', None, 'col')
Inputs may be any that keep to these rules, and one draw needn't show every extreme that they name: `near_ids`: slot 0 of cluster i names its sibling: i + 2 when i // 2 is even, else i - 2. The other slots may name any cluster. For sibling clusters a and b = a + 2 (a // 2 even), near_blocks[b, 0] is the transpose of near_blocks[a, 0]. `diag_blocks`: Symmetric. `cluster_bases`: the identity plus a small full-rank perturbation. `parent_bases`: the identity plus a small full-rank perturbation.
All inputs are finite; a program needn't handle non-finite values.
Results may differ from a plain program's by a relative error of at most 0.0003.
Values sent between devices are 32-bit elements; how exact they have to be, the bound alone decides.
No kernel may reach another device: no remote copies, remote signals or barrier semaphores. Data moves between devices by JAX's collectives and lax.ppermute only.
A program may use at most 128 MiB of HBM per device.

v0:
```python
import jax
import jax.numpy as jnp
from jax import lax
from jax.sharding import PartitionSpec as P

B = 512
K = 256
NEAR = 4
highest = lax.Precision.HIGHEST


def partner(shard, axis, apart):
    return lax.ppermute(shard, axis, [(i, i ^ 1 << apart) for i in range(lax.axis_size(axis))])


def eliminate(dense, redundant):
    factor = jnp.linalg.cholesky(dense[:redundant, :redundant])
    solved = jax.scipy.linalg.cho_solve((factor, True), dense[:redundant, redundant:])
    schur = dense[redundant:, redundant:] - jnp.dot(
        dense[redundant:, :redundant], solved, precision=highest
    )
    return (solved, schur)


def per_device(diag_blocks, near_blocks, cluster_bases, near_ids, near_count, parent_bases):
    clusters = diag_blocks.shape[0]
    redundant = B - K
    column = lax.axis_index("col")
    quarter = K // lax.axis_size("col")
    own_rows = cluster_bases.shape[1]
    full_bases = lax.all_gather(cluster_bases, "col", axis=1, tiled=True)
    partial_value = jnp.einsum("cij,cjk->cik", diag_blocks, cluster_bases, precision=highest)
    summed = lax.psum(partial_value, "col")
    dense = jnp.einsum("cji,cjk->cik", full_bases, summed, precision=highest)
    solved, schur = jax.vmap(lambda single: eliminate(single, redundant))(dense)
    leaf_diag = lax.dynamic_slice_in_dim(schur, column * quarter, quarter, 2)
    flat_ids = near_ids.reshape(-1)
    shards = lax.all_gather(cluster_bases[:, :, redundant:], "row", axis=0, tiled=True)
    number = shards.shape[0]
    one_hot = (flat_ids[:, None] == jnp.arange(number, dtype=jnp.int32)[None, :]).astype(
        jnp.float32
    )
    picked = jnp.dot(one_hot, shards.reshape(number, -1), precision=highest)
    picked = picked.reshape(clusters, NEAR, own_rows, K)
    terms = jnp.einsum("cnij,cnjk->cnik", near_blocks, picked, precision=highest)
    right_part = lax.psum_scatter(terms, "col", scatter_dimension=3, tiled=True)
    moved = jnp.einsum("cji,cnjk->cnik", full_bases, right_part, precision=highest)
    coupled = moved[:, :, redundant:, :] - jnp.einsum(
        "cri,cnrk->cnik", solved, moved[:, :, :redundant, :], precision=highest
    )
    live = (jnp.arange(NEAR, dtype=jnp.int32)[None, :] < near_count[:, None]).astype(jnp.float32)
    leaf_near = coupled * live[:, :, None, None]
    halfway = clusters // 2
    parity = lax.axis_index("row") % 2
    stacked = jnp.stack([leaf_diag, leaf_near[:, 0]])
    kept = lax.dynamic_slice_in_dim(stacked, parity * halfway, halfway, 1)
    outgoing = lax.dynamic_slice_in_dim(stacked, (1 - parity) * halfway, halfway, 1)
    arrived = partner(outgoing, "row", 0)
    first_child = jnp.where(parity == 0, kept, arrived)
    second_child = jnp.where(parity == 0, arrived, kept)
    left_columns = jnp.concatenate([first_child[0], second_child[1]], axis=1)
    right_columns = jnp.concatenate([first_child[1], second_child[0]], axis=1)
    merged = jnp.concatenate([left_columns, right_columns], axis=2)
    rows_first = lax.dynamic_slice_in_dim(parent_bases, column * quarter, quarter, 1)
    rows_second = lax.dynamic_slice_in_dim(parent_bases, K + column * quarter, quarter, 1)
    chosen_rows = jnp.concatenate([rows_first, rows_second], axis=1)
    lifted = jnp.einsum("hji,hjk->hik", parent_bases, merged, precision=highest)
    parent_part = jnp.einsum("hij,hjk->hik", lifted, chosen_rows, precision=highest)
    parent_dense = lax.psum(parent_part, "col")
    parent_schur = jax.vmap(lambda single: eliminate(single, K)[1])(parent_dense)
    parent_diag = lax.dynamic_slice_in_dim(parent_schur, column * quarter, quarter, 2)
    return (leaf_diag, leaf_near, parent_diag)


def solution(mesh):
    return jax.shard_map(
        per_device,
        mesh=mesh,
        in_specs=(
            P("row", None, "col"),
            P("row", None, None, "col"),
            P("row", "col", None),
            P("row", None),
            P("row"),
            P("row", None, None),
        ),
        out_specs=(P("row", None, "col"), P("row", None, None, "col"), P("row", None, "col")),
        check_vma=False,
    )
```

profile of v0, /device:TPU:0, one launch (start us, length us, event | category | flops | bytes accessed | tf_op | source)
XLA Modules:
  0.0 401.4 jit_solution(10855884119777863552)
XLA Ops:
  8.1 1.8 slice.175
  9.9 4.4 %fusion.60 = f32[2,512,512]{2,1,0:T(8,128)} fusion(f32[2,512,128]{2,1,0:T(8,128)} %param.6, f32[2,128,512]{2,1,0:T(8,128)} %param.8), kind=kOutput, calls=%fused_computation.129 | convolution fusion | flops 805306368 | bytes 3145728 | tf_op jit(solution)/shard_map/cij,cjk->cik/dot_general | solution.py:32
  15.1 26.7 %all-gather.5.cloned.1.call-done = f32[16,128,256]{2,1,0:T(8,128)} async-done(((f32[2,128,256]{2,1,0:T(8,128)}), f32[16,128,256]{2,1,0:T(8,128)}) %all-gather.5.cloned.1.call-update) | async-done | bytes 2097168 | tf_op jit(solution)/shard_map/all_gather | solution.py:38
  41.8 3.8 fusion
  45.7 5.1 %convolution_bitcast_fusion = f32[2,4,512,256]{2,3,1,0:T(8,128)} fusion(f32[2,4,512,128]{3,2,1,0:T(8,128)S(1)} %copy-done, f32[2,4,128,256]{3,1,2,0:T(4,128)S(1)} %fusion), kind=kOutput, calls=%fused_computation.4 | convolution fusion | flops 1610612736 | bytes 7340032 | tf_op jit(solution)/shard_map/cnij,cnjk->cnik/dot_general | solution.py:45
  51.5 75.6 %all-reduce.5.cloned.1.call-done = f32[2,512,512]{2,1,0:T(8,128)} async-done(((f32[2,512,512]{2,1,0:T(8,128)}), f32[2,512,512]{2,1,0:T(8,128)}) %all-reduce.5.cloned.1.call-update) | async-done | bytes 2097168 | tf_op jit(solution)/shard_map/psum | solution.py:33
  127.1 5.7 %convolution_bitcast_fusion.1 = f32[2,512,512]{1,2,0:T(8,128)S(1)} fusion(f32[2,512,512]{2,1,0:T(8,128)} %all-reduce.5.cloned.1.call-done, f32[2,512,512]{2,1,0:T(8,128)} %all-gather.3.cloned.1.call-done), kind=kOutput, calls=%fused_computation.10 | convolution fusion | flops 3221225472 | bytes 6291456 | tf_op jit(solution)/shard_map/cji,cjk->cik/dot_general | solution.py:34
  132.8 1.3 copy-done.1
  137.3 23.9 %custom-call.40 = f32[2,128,128]{2,1,0:T(8,128)S(1)} custom-call(f32[2,128,128]{2,1,0:T(8,128)S(1)} %cholesky.239), custom_call_target="Cholesky" | custom-call | tf_op jit(solution)/shard_map/vmap(jit(cholesky))/cholesky | solution.py:17
  161.3 19.7 %custom-call.41 = f32[2,1,128,128]{2,3,1,0:T(8,128)S(1)} custom-call(f32[2,1,128,128]{3,2,1,0:T(8,128)S(1)} %select_bitcast_fusion), custom_call_target="InvertDiagBlocksLowerTriangular" | custom-call | tf_op jit(solution)/shard_map/vmap(jit(cholesky))/cholesky | solution.py:17
  180.9 1.2 constant_dynamic-update-slice_fusion.2
  182.1 1.3 convolution_subtract_fusion.3
  183.4 23.5 %custom-call.42 = f32[2,128,128]{2,1,0:T(8,128)S(1)} custom-call(f32[2,128,128]{2,1,0:T(8,128)S(1)} %convolution_subtract_fusion.3), custom_call_target="Cholesky" | custom-call | tf_op jit(solution)/shard_map/vmap(jit(cholesky))/cholesky | solution.py:17
  207.3 3.9 while.2
  208.0 1.3 bitcast_dynamic-update-slice_fusion.5
  209.9 1.3 bitcast_dynamic-update-slice_fusion.5
  211.2 39.5 %custom-call.43 = f32[2,2,128,128]{2,3,1,0:T(8,128)S(1)} custom-call(f32[2,2,128,128]{3,2,1,0:T(8,128)S(1)} %bitcast.192), custom_call_target="InvertDiagBlocksLowerTriangular" | custom-call | tf_op jit(solution)/shard_map/vmap(jit(_cho_solve))/triangular_solve | solution.py:18
  250.7 1.4 fusion.20
  252.1 1.6 convolution_subtract_fusion.1
  255.3 2.1 fusion.16
  258.4 3.9 fusion.4
  267.0 2.0 convolution_bitcast_fusion.2
  269.1 51.3 %all-reduce.7.cloned.1.call-done = f32[1,512,512]{1,2,0:T(8,128)} async-done(((f32[1,512,512]{1,2,0:T(8,128)}), f32[1,512,512]{1,2,0:T(8,128)}) %all-reduce.7.cloned.1.call-update) | async-done | bytes 1048592 | tf_op jit(solution)/shard_map/psum | solution.py:69
  320.4 1.9 fusion.59
  325.2 11.7 %custom-call.44 = f32[1,128,128]{2,1,0:T(8,128)S(1)} custom-call(f32[1,128,128]{2,1,0:T(8,128)S(1)} %cholesky.242), custom_call_target="Cholesky" | custom-call | tf_op jit(solution)/shard_map/vmap(jit(cholesky))/cholesky | solution.py:17
  337.0 10.0 %custom-call.45 = f32[1,1,128,128]{2,3,1,0:T(8,128)S(1)} custom-call(f32[1,1,128,128]{3,2,1,0:T(8,128)S(1)} %get-tuple-element.57), custom_call_target="InvertDiagBlocksLowerTriangular" | custom-call | tf_op jit(solution)/shard_map/vmap(jit(cholesky))/cholesky | solution.py:17
  349.1 11.7 %custom-call.46 = f32[1,128,128]{2,1,0:T(8,128)S(1)} custom-call(f32[1,128,128]{2,1,0:T(8,128)S(1)} %fusion.11), custom_call_target="Cholesky" | custom-call | tf_op jit(solution)/shard_map/vmap(jit(cholesky))/cholesky | solution.py:17
  364.3 5.3 %while.3 = (s32[]{:T(128)}, f32[1,256,256]{2,1,0:T(8,128)S(1)}, s32[2,2]{1,0:T(2,128)S(1)}, f32[2,1,128,128]{3,2,1,0:T(8,128)}, s32[]{:T(128)}) while((s32[]{:T(128)}, f32[1,256,256]{2,1,0:T(8,128)S(1)}, s32[2,2]{1,0:T(2,128)S(1)}, f32[2,1,128,128]{3,2,1,0:T(8,128)}, s32[]{:T(128)}) %tuple.66), condition=%wide.while_cond.1, body=%wide.while_body.1.sunk | while | flops 2 | bytes 132205 | solution.py:18
  365.0 2.0 bitcast_dynamic-update-slice_fusion.6
  367.6 2.0 bitcast_dynamic-update-slice_fusion.6
  369.6 20.5 %custom-call.47 = f32[1,2,128,128]{2,3,1,0:T(8,128)S(1)} custom-call(f32[1,2,128,128]{3,2,1,0:T(8,128)} %bitcast.193), custom_call_target="InvertDiagBlocksLowerTriangular" | custom-call | tf_op jit(solution)/shard_map/vmap(jit(_cho_solve))/triangular_solve | solution.py:18
  392.6 1.5 dynamic-slice_subtract_fusion.1
  (92 shorter events, 24.7 us)
Async XLA Ops:
  8.0 37.7 %copy-start = (f32[2,4,512,128]{3,2,1,0:T(8,128)S(1)}, f32[2,4,512,128]{3,2,1,0:T(8,128)}, u32[]{:S(2)}) copy-start(f32[2,4,512,128]{3,2,1,0:T(8,128)} %param.7) | copy-start | bytes 6291460
  8.0 33.8 %all-gather.5.cloned.1.call-start = ((), (), s32[]{:S(2)}) async-start(), calls=%async_computation.3 | async-start | bytes 2359296 | tf_op jit(solution)/shard_map/all_gather | solution.py:38
  9.9 117.2 %all-reduce.5.cloned.1.call-start = ((), (), s32[]{:S(2)}) async-start(), calls=%async_computation.1 | async-start | bytes 4194304 | tf_op jit(solution)/shard_map/psum | solution.py:33
  14.3 27.5 %copy-start.9 = (s32[2,4]{1,0:T(2,128)S(1)}, s32[2,4]{1,0:T(2,128)}, u32[]{:S(2)}) copy-start(s32[2,4]{1,0:T(2,128)} %param.9) | copy-start | bytes 100
  14.3 112.8 %all-gather.3.cloned.1.call-start = ((), (), s32[]{:S(2)}) async-start(), calls=%async_computation.2 | async-start | bytes 2621440 | tf_op jit(solution)/shard_map/all_gather | solution.py:31
  15.1 243.3 %reduce-scatter.2.cloned.1.call-start = ((), (), s32[]{:S(2)}) async-start(), calls=%async_computation.4 | async-start | bytes 5242880 | tf_op jit(solution)/shard_map/reduce_scatter | solution.py:46
  50.8 0.7 copy-start.10
  50.8 269.6 %all-reduce.7.cloned.1.call-start = ((), (), s32[]{:S(2)}) async-start(), calls=%async_computation.5 | async-start | bytes 2097152 | tf_op jit(solution)/shard_map/psum | solution.py:69
  132.8 1.3 copy-start.1
  136.4 0.8 copy-start.4
  258.3 7.0 %copy-start.5 = (f32[2,256,64]{1,2,0:T(8,128)}, f32[2,256,64]{1,2,0:T(8,128)S(1)}, u32[]{:S(2)}) copy-start(f32[2,256,64]{1,2,0:T(8,128)S(1)} %dynamic-slice_subtract_fusion) | copy-start | bytes 393220
  262.9 0.8 copy-start.7
  263.7 2.6 copy-start.3
  263.8 1.5 collective-permute-start
  322.3 67.8 %copy-start.2 = (f32[1,512,512]{1,2,0:T(8,128)S(1)}, f32[1,512,512]{1,2,0:T(8,128)}, u32[]{:S(2)}) copy-start(f32[1,512,512]{1,2,0:T(8,128)} %all-reduce.7.cloned.1.call-done) | copy-start | bytes 3145732
  324.5 0.7 copy-start.8
  361.5 1.9 copy-start.6
Sparse Core Ops, SparseCore 0:
  11.3 30.4 all-gather.4
  43.4 72.8 all-gather.2
  269.2 51.1 all-reduce.6
Sparse Core Ops, SparseCore 1:
  14.4 112.6 all-reduce.4
  129.3 75.8 reduce-scatter.1
where the time goes:
time: 410 us; the launch traced here: 401 us
  other arithmetic  169 us (41%)
  waiting for transfers between devices  155 us (38%)
  matrix products  40 us (10%)
  local copies, waits for them, and re-layouts  20.5 us (5%)
  between operations  17.1 us (4%)
    another operation x16, other arithmetic, eliminate(): factor = jnp.linalg.cholesky(dense[:redundant, :redundant])  102 us
    psum x1, waiting for transfers between devices, per_device(): summed = lax.psum(partial_value, 'col')  75.6 us
    another operation x6, other arithmetic, eliminate(): jax.scipy.linalg.cho_solve((factor, True), dense[:redundant, redundant:])  61.1 us
    psum x1, waiting for transfers between devices, per_device(): parent_dense = lax.psum(parent_part, 'col')  51.3 us
    all_gather x1, waiting for transfers between devices, per_device(): lax.all_gather(cluster_bases[:, :, redundant:], 'row', axis=0, tiled=True)  26.7 us
    another operation x12, local copies, waits for them, and re-layouts  9.11 us
  transfers between devices with their start and end apart: 6, of which 4 were waited for; matrix products, arithmetic and copies ran while one was open for 36% of the time, Pallas kernels for 0%

commit v1 on v0

--- a/solution.py
+++ b/solution.py
@@ -30,7 +30,7 @@
     own_rows = cluster_bases.shape[1]
     full_bases = lax.all_gather(cluster_bases, "col", axis=1, tiled=True)
     partial_value = jnp.einsum("cij,cjk->cik", diag_blocks, cluster_bases, precision=highest)
-    summed = lax.psum(partial_value, "col")
+    summed = jnp.sum(lax.all_gather(partial_value, "col"), axis=0)
     dense = jnp.einsum("cji,cjk->cik", full_bases, summed, precision=highest)
     solved, schur = jax.vmap(lambda single: eliminate(single, redundant))(dense)
     leaf_diag = lax.dynamic_slice_in_dim(schur, column * quarter, quarter, 2)

time: 410 us -> 597 us (1.46)
  waiting for transfers between devices: 155 us -> 341 us
  other arithmetic: 169 us -> 175 us
    all_gather x0 -> x1, waiting for transfers between devices: none -> 147 us  [per_device(): summed = jnp.sum(lax.all_gather(partial_value, 'col'), axis=0)]
    reduce_scatter x1, waiting for transfers between devices: 0.03 us -> 77.9 us  [per_device(): right_part = lax.psum_scatter(terms, 'col', scatter_dimension=3, tiled=True)]
    psum x1 -> x0, waiting for transfers between devices: 75.6 us -> none  [per_device(): summed = lax.psum(partial_value, 'col')]
    all_gather x1, waiting for transfers between devices: 0.01 us -> 33.2 us  [per_device(): full_bases = lax.all_gather(cluster_bases, 'col', axis=1, tiled=True)]
    reduce_sum x0 -> x1, other arithmetic: none -> 6.02 us  [per_device(): summed = jnp.sum(lax.all_gather(partial_value, 'col'), axis=0)]
  transfers between devices with their start and end apart: 6 -> 6, of which waited for: 4 -> 6; matrix products, arithmetic and copies ran while one was open for 36% -> 3% of each run, Pallas kernels for 0% -> 0%
where the time goes in v1:
time: 597 us; the launch traced here: 592 us
  waiting for transfers between devices  341 us (57%)
  other arithmetic  175 us (29%)
  matrix products  40 us (7%)
  local copies, waits for them, and re-layouts  19 us (3%)
  between operations  16.1 us (3%)
    all_gather x1, waiting for transfers between devices, per_device(): summed = jnp.sum(lax.all_gather(partial_value, 'col'), axis=0)  147 us
    another operation x16, other arithmetic, eliminate(): factor = jnp.linalg.cholesky(dense[:redundant, :redundant])  102 us
    reduce_scatter x1, waiting for transfers between devices, per_device(): right_part = lax.psum_scatter(terms, 'col', scatter_dimension=3, tiled=True)  77.9 us
    another operation x6, other arithmetic, eliminate(): jax.scipy.linalg.cho_solve((factor, True), dense[:redundant, redundant:])  61.2 us
    psum x1, waiting for transfers between devices, per_device(): parent_dense = lax.psum(parent_part, 'col')  50.2 us
    all_gather x1, waiting for transfers between devices, per_device(): full_bases = lax.all_gather(cluster_bases, 'col', axis=1, tiled=True)  33.2 us
    all_gather x1, waiting for transfers between devices, per_device(): lax.all_gather(cluster_bases[:, :, redundant:], 'row', axis=0, tiled=True)  31.1 us
  transfers between devices with their start and end apart: 6, of which 6 were waited for; matrix products, arithmetic and copies ran while one was open for 3% of the time, Pallas kernels for 0%

profile of v1, /device:TPU:0, one launch (start us, length us, event | category | flops | bytes accessed | tf_op | source)
XLA Modules:
  0.0 591.9 jit_solution(2076798502497142621)
XLA Ops:
  7.2 1.8 slice.175
  9.9 31.1 %all-gather.7.cloned.1.call-done = f32[16,128,256]{2,1,0:T(8,128)} async-done(((f32[2,128,256]{2,1,0:T(8,128)}), f32[16,128,256]{2,1,0:T(8,128)}) %all-gather.7.cloned.1.call-update) | async-done | bytes 2097168 | tf_op jit(solution)/shard_map/all_gather | solution.py:38
  41.0 3.8 fusion
  44.8 5.1 convolution_bitcast_fusion
  51.2 3.1 fusion.60
  55.1 33.2 %all-gather.5.cloned.1.call-done = f32[2,512,512]{2,1,0:T(8,128)} async-done(((f32[2,128,512]{2,1,0:T(8,128)}), f32[2,512,512]{2,1,0:T(8,128)}) %all-gather.5.cloned.1.call-update) | async-done | bytes 2097168 | tf_op jit(solution)/shard_map/all_gather | solution.py:31
  88.2 77.9 %reduce-scatter.2.cloned.1.call-done = f32[2,4,512,64]{2,3,1,0:T(8,128)} async-done(((f32[2,4,512,256]{2,3,1,0:T(8,128)}), f32[2,4,512,64]{2,3,1,0:T(8,128)}) %reduce-scatter.2.cloned.1.call-update) | async-done | bytes 1048592 | tf_op jit(solution)/shard_map/reduce_scatter | solution.py:46
  166.2 4.8 fusion.4
  171.0 146.7 %all-gather.9.cloned.1.call-done = f32[8,512,512]{2,1,0:T(8,128)} async-done(((f32[2,512,512]{2,1,0:T(8,128)}), f32[8,512,512]{2,1,0:T(8,128)}) %all-gather.9.cloned.1.call-update) | async-done | bytes 8388624 | tf_op jit(solution)/shard_map/all_gather | solution.py:33
  317.8 6.0 %reduce_sum.9 = f32[2,512,512]{2,1,0:T(8,128)} reduce(f32[4,2,512,512]{3,2,1,0:T(8,128)} %bitcast.189, f32[]{:T(128)} %constant.207.clone.1), dimensions={0}, to_apply=%region_0.0 | reduce | flops 1572864 | bytes 10485764 | tf_op jit(solution)/shard_map/reduce_sum | solution.py:33
  323.8 5.7 convolution_bitcast_fusion.1
  333.9 23.6 %custom-call.40 = f32[2,128,128]{2,1,0:T(8,128)S(1)} custom-call(f32[2,128,128]{2,1,0:T(8,128)S(1)} %cholesky.239), custom_call_target="Cholesky" | custom-call | tf_op jit(solution)/shard_map/vmap(jit(cholesky))/cholesky | solution.py:17
  357.6 19.7 %custom-call.41 = f32[2,1,128,128]{2,3,1,0:T(8,128)S(1)} custom-call(f32[2,1,128,128]{3,2,1,0:T(8,128)S(1)} %select_bitcast_fusion), custom_call_target="InvertDiagBlocksLowerTriangular" | custom-call | tf_op jit(solution)/shard_map/vmap(jit(cholesky))/cholesky | solution.py:17
  379.8 23.5 %custom-call.42 = f32[2,128,128]{2,1,0:T(8,128)S(1)} custom-call(f32[2,128,128]{2,1,0:T(8,128)S(1)} %convolution_subtract_fusion.3), custom_call_target="Cholesky" | custom-call | tf_op jit(solution)/shard_map/vmap(jit(cholesky))/cholesky | solution.py:17
  403.6 3.9 while.2
  407.5 39.5 %custom-call.43 = f32[2,2,128,128]{2,3,1,0:T(8,128)S(1)} custom-call(f32[2,2,128,128]{3,2,1,0:T(8,128)S(1)} %bitcast.194), custom_call_target="InvertDiagBlocksLowerTriangular" | custom-call | tf_op jit(solution)/shard_map/vmap(jit(_cho_solve))/triangular_solve | solution.py:18
  447.1 1.4 fusion.20
  448.5 1.6 convolution_subtract_fusion.1
  451.6 2.2 fusion.16
  455.8 1.4 collective-permute-done
  458.9 2.0 convolution_bitcast_fusion.2
  461.0 50.2 %all-reduce.4.cloned.1.call-done = f32[1,512,512]{1,2,0:T(8,128)} async-done(((f32[1,512,512]{1,2,0:T(8,128)}), f32[1,512,512]{1,2,0:T(8,128)}) %all-reduce.4.cloned.1.call-update) | async-done | bytes 1048592 | tf_op jit(solution)/shard_map/psum | solution.py:69
  511.2 1.9 fusion.59
  515.9 11.7 %custom-call.44 = f32[1,128,128]{2,1,0:T(8,128)S(1)} custom-call(f32[1,128,128]{2,1,0:T(8,128)S(1)} %cholesky.242), custom_call_target="Cholesky" | custom-call | tf_op jit(solution)/shard_map/vmap(jit(cholesky))/cholesky | solution.py:17
  527.7 9.8 %custom-call.45 = f32[1,1,128,128]{2,3,1,0:T(8,128)S(1)} custom-call(f32[1,1,128,128]{3,2,1,0:T(8,128)S(1)} %get-tuple-element.57), custom_call_target="InvertDiagBlocksLowerTriangular" | custom-call | tf_op jit(solution)/shard_map/vmap(jit(cholesky))/cholesky | solution.py:17
  538.6 1.3 fusion.11
  539.9 11.7 %custom-call.46 = f32[1,128,128]{2,1,0:T(8,128)S(1)} custom-call(f32[1,128,128]{2,1,0:T(8,128)S(1)} %fusion.11), custom_call_target="Cholesky" | custom-call | tf_op jit(solution)/shard_map/vmap(jit(cholesky))/cholesky | solution.py:17
  555.4 5.1 while.3
  556.0 1.9 bitcast_dynamic-update-slice_fusion.6
  558.5 1.9 bitcast_dynamic-update-slice_fusion.6
  560.4 20.5 %custom-call.47 = f32[1,2,128,128]{2,3,1,0:T(8,128)S(1)} custom-call(f32[1,2,128,128]{3,2,1,0:T(8,128)} %bitcast.195), custom_call_target="InvertDiagBlocksLowerTriangular" | custom-call | tf_op jit(solution)/shard_map/vmap(jit(_cho_solve))/triangular_solve | solution.py:18
  583.5 1.5 dynamic-slice_subtract_fusion.1
  (97 shorter events, 29.1 us)
Async XLA Ops:
  7.2 37.7 %copy-start = (f32[2,4,512,128]{3,2,1,0:T(8,128)S(1)}, f32[2,4,512,128]{3,2,1,0:T(8,128)}, u32[]{:S(2)}) copy-start(f32[2,4,512,128]{3,2,1,0:T(8,128)} %param.7) | copy-start | bytes 6291460
  7.2 33.8 %all-gather.7.cloned.1.call-start = ((), (), s32[]{:S(2)}) async-start(), calls=%async_computation.2 | async-start | bytes 2359296 | tf_op jit(solution)/shard_map/all_gather | solution.py:38
  9.1 79.2 %all-gather.5.cloned.1.call-start = ((), (), s32[]{:S(2)}) async-start(), calls=%async_computation.1 | async-start | bytes 2621440 | tf_op jit(solution)/shard_map/all_gather | solution.py:31
  9.8 156.4 %reduce-scatter.2.cloned.1.call-start = ((), (), s32[]{:S(2)}) async-start(), calls=%async_computation.3 | async-start | bytes 5242880 | tf_op jit(solution)/shard_map/reduce_scatter | solution.py:46
  50.0 1.1 copy-start.2
  50.0 1.2 copy-start.11
  50.0 5.0 copy-start.12
  50.0 267.8 %all-gather.9.cloned.1.call-start = ((), (), s32[]{:S(2)}) async-start(), calls=%async_computation.5 | async-start | bytes 10485760 | tf_op jit(solution)/shard_map/all_gather | solution.py:33
  54.3 456.9 %all-reduce.4.cloned.1.call-start = ((), (), s32[]{:S(2)}) async-start(), calls=%async_computation.4 | async-start | bytes 2097152 | tf_op jit(solution)/shard_map/psum | solution.py:69
  329.5 1.3 copy-start.1
  333.1 0.8 copy-start.6
  450.0 3.8 copy-start.3
  451.6 4.1 copy-start.5
  454.5 1.1 copy-start.9
  455.6 5.3 copy-start.7
  455.7 1.5 collective-permute-start
  513.1 67.9 %copy-start.4 = (f32[1,512,512]{1,2,0:T(8,128)S(1)}, f32[1,512,512]{1,2,0:T(8,128)}, u32[]{:S(2)}) copy-start(f32[1,512,512]{1,2,0:T(8,128)} %all-reduce.4.cloned.1.call-done) | copy-start | bytes 3145732
  515.2 0.7 copy-start.10
  552.3 2.0 copy-start.8
Sparse Core Ops, SparseCore 0:
  10.4 30.4 all-gather.6
  42.6 45.6 all-gather.4
  90.5 75.5 reduce-scatter.1
  167.6 150.1 all-gather.8
  461.1 50.0 all-reduce.3
